TPU v7x, 32 devices: a whole 2x2x4 slice. The times are simulated.
32 devices in a mesh: dp: 4 (over x, core), fsdp: 8 (over z, y).
Axes of the slice: x: 2, y: 2, z: 4, core: 2. Of those that a mesh axis runs over, the one named last changes fastest.
Arguments:
- tokens: bfloat16 [64, 512, 768], P(('dp', 'fsdp')), may hold values from -6 to 6
- segment_ids: int32 [64, 512], P(('dp', 'fsdp')), may hold values from 0 to 32, as said below
- qkv_weight: bfloat16 [768, 576], P(('dp', 'fsdp')), may hold values from -0.4375 to 0.4375
- out_weight: bfloat16 [768, 768], P(('dp', 'fsdp')), may hold values from -2.5 to 2.5
- up_weight: bfloat16 [768, 768], P(('dp', 'fsdp')), may hold values from -0.4375 to 0.4375
- down_weight: bfloat16 [3072, 192], P(('dp', 'fsdp')), may hold values from -0.21875 to 0.21875
- biases: bfloat16 [6, 768], P(None, ('dp', 'fsdp')), may hold values from -1 to 1
- up_bias: bfloat16 [3072], P(('dp', 'fsdp')), may hold values from -2.5 to 2.5
- gains: bfloat16 [2, 768], P(None, ('dp', 'fsdp')), may hold values from 0.5 to 1.5
- cotangent: bfloat16 [64, 512, 768], P(('dp', 'fsdp')), may hold values from -6 to 6
Outputs:
- layer_out: bfloat16 [64, 512, 768], P(('dp', 'fsdp'))
- input_grad: float32 [64, 512, 768], P(('dp', 'fsdp'))
- qkv_grad: float32 [768, 576], P(('dp', 'fsdp'))
- out_grad: float32 [768, 768], P(('dp', 'fsdp'))
- up_grad: float32 [768, 768], P(('dp', 'fsdp'))
- down_grad: float32 [3072, 192], P(('dp', 'fsdp'))
- bias_grad: float32 [6, 768], P(None, ('dp', 'fsdp'))
- up_bias_grad: float32 [3072], P(('dp', 'fsdp'))
- gain_grad: float32 [2, 768], P(None, ('dp', 'fsdp'))
Inputs may be any that keep to these rules, and one draw needn't show every extreme that they name: `segment_ids`: in each row the real tokens carry document numbers from 1 upward that never fall, each document contiguous; after them come 0 to 64 padding tokens numbered 0, exactly 64 in the first row.
All inputs are finite; a program needn't handle non-finite values.
Results may differ from a plain program's by a relative error of at most 0.012.
The roundings to bfloat16 on the way count: a program that leaves them out, or rounds other values in their place, can miss the bound.
Values may be sent and summed in bfloat16 or wider, within the bound.
A program may use at most 128 MiB of HBM per device.

v0:
```python
from functools import partial

import jax
import jax.numpy as jnp
from jax import lax
from jax.sharding import PartitionSpec as P

HEADS = 12
GROUPS = 4


EPSILON = 1e-05
SCORE_SCALE = 0.125
NEG_FILL = -1e30


def group_apply(values, weight):
    parts = values.reshape(values.shape[0], GROUPS, -1)
    table = weight.reshape(GROUPS, parts.shape[2], -1)
    return jnp.einsum("ngc,gce->nge", parts, table, preferred_element_type=jnp.float32)


def normalize(hidden):
    centre = hidden - jnp.mean(hidden, -1, keepdims=True)
    spread = lax.rsqrt(jnp.mean(centre * centre, -1, keepdims=True) + EPSILON)
    return (centre * spread, spread)


def norm_back(upstream, gain, normed, spread):
    scaled = upstream * gain
    return spread * (
        scaled
        - jnp.mean(scaled, -1, keepdims=True)
        - normed * jnp.mean(scaled * normed, -1, keepdims=True)
    )


def block_scores(query_blk, keys_seq, seg_blk, seg_seq):
    raw = (
        jnp.einsum("qhd,khd->hqk", query_blk, keys_seq, preferred_element_type=jnp.float32)
        * SCORE_SCALE
    )
    allowed = (seg_seq != 0)[None, :] & (
        (seg_blk[:, None] == seg_seq[None, :]) | (seg_blk[:, None] == 0)
    )
    return jnp.where(allowed[None], raw, NEG_FILL)


def attend_forward(item):
    queries_s, keys_s, values_s, seg_s = item
    pieces, sums_log = ([], [])
    scores = block_scores(queries_s, keys_s, seg_s, seg_s)
    top = jnp.max(scores, -1, keepdims=True)
    expd = jnp.exp(scores - top)
    total = jnp.sum(expd, -1, keepdims=True)
    probs = (expd / total).astype(jnp.bfloat16)
    pieces.append(jnp.einsum("hqk,khd->qhd", probs, values_s, preferred_element_type=jnp.float32))
    sums_log.append((top + jnp.log(total))[..., 0])
    return (jnp.concatenate(pieces, 0), jnp.concatenate(sums_log, 1))


def attend_backward(item):
    queries_s, keys_s, values_s, seg_s, lse_s, grad_ctx_s = item
    length = queries_s.shape[0]
    block_rows = min(512, length)
    grad_keys = jnp.zeros(keys_s.shape, jnp.float32)
    grad_values = jnp.zeros(values_s.shape, jnp.float32)
    scores = block_scores(queries_s, keys_s, seg_s, seg_s)
    probs = jnp.exp(scores - lse_s[:, 0:block_rows, None])
    grad_values = grad_values + jnp.einsum(
        "hqk,qhd->khd", probs.astype(jnp.bfloat16), grad_ctx_s, preferred_element_type=jnp.float32
    )
    grad_probs = jnp.einsum(
        "qhd,khd->hqk", grad_ctx_s, values_s, preferred_element_type=jnp.float32
    )
    inner = jnp.sum(probs * grad_probs, -1, keepdims=True)
    grad_scores = (probs * (grad_probs - inner)).astype(jnp.bfloat16)
    query_parts = [
        jnp.einsum("hqk,khd->qhd", grad_scores, keys_s, preferred_element_type=jnp.float32)
        * SCORE_SCALE
    ]
    grad_keys = (
        grad_keys
        + jnp.einsum("hqk,qhd->khd", grad_scores, queries_s, preferred_element_type=jnp.float32)
        * SCORE_SCALE
    )
    return (jnp.concatenate(query_parts, 0), grad_keys, grad_values)


def reduce_ffn(up_grad, down_grad, up_bias_grad):
    return (
        lax.psum_scatter(up_grad, ("dp", "fsdp"), scatter_dimension=0, tiled=True),
        lax.psum_scatter(down_grad, ("dp", "fsdp"), scatter_dimension=0, tiled=True),
        lax.psum_scatter(up_bias_grad, ("dp", "fsdp"), scatter_dimension=0, tiled=True),
    )


def local(
    tokens,
    segment_ids,
    qkv_weight,
    out_weight,
    up_weight,
    down_weight,
    biases,
    up_bias,
    gains,
    cotangent,
):

    def fetch_attention():
        return (
            lax.all_gather(qkv_weight, ("dp", "fsdp"), axis=0, tiled=True),
            lax.all_gather(out_weight, ("dp", "fsdp"), axis=0, tiled=True),
            lax.all_gather(biases, ("dp", "fsdp"), axis=1, tiled=True),
            lax.all_gather(gains, ("dp", "fsdp"), axis=1, tiled=True),
        )

    def fetch_ffn():
        return (
            lax.all_gather(up_weight, ("dp", "fsdp"), axis=0, tiled=True),
            lax.all_gather(down_weight, ("dp", "fsdp"), axis=0, tiled=True),
            lax.all_gather(up_bias, ("dp", "fsdp"), axis=0, tiled=True),
        )

    qkv_full, out_full, bias_full, gain_full = fetch_attention()
    up_full, down_full, up_bias_full = fetch_ffn()
    count, length, width = tokens.shape
    rows = count * length
    group_w = width // GROUPS
    shape4 = (count, length, HEADS, width // HEADS)
    inputs = tokens.reshape(rows, width)
    bias_vals = bias_full.astype(jnp.float32)
    gain_vals = gain_full.astype(jnp.float32)
    mixed = group_apply(inputs, qkv_full)
    queries = (
        (mixed[:, :, :group_w].reshape(rows, width) + bias_vals[0])
        .astype(jnp.bfloat16)
        .reshape(shape4)
    )
    keys_all = (
        mixed[:, :, group_w : 2 * group_w].reshape(rows, width).astype(jnp.bfloat16).reshape(shape4)
    )
    values_all = (
        (mixed[:, :, 2 * group_w :].reshape(rows, width) + bias_vals[1])
        .astype(jnp.bfloat16)
        .reshape(shape4)
    )
    attended, lse = lax.map(attend_forward, (queries, keys_all, values_all, segment_ids))
    context = attended.reshape(rows, width).astype(jnp.bfloat16)
    hidden1 = (
        inputs.astype(jnp.float32)
        + jnp.dot(context, out_full, preferred_element_type=jnp.float32)
        + bias_vals[2]
    )
    normed1, spread1 = normalize(hidden1)
    layer1 = normed1 * gain_vals[0] + bias_vals[3]
    layer1_low = layer1.astype(jnp.bfloat16)
    pre_act = group_apply(layer1_low, up_full).reshape(rows, -1) + up_bias_full.astype(jnp.float32)
    activ, gelu_pull = jax.vjp(partial(jax.nn.gelu, approximate=False), pre_act)
    activ_low = activ.astype(jnp.bfloat16)
    hidden2 = layer1 + group_apply(activ_low, down_full).reshape(rows, width) + bias_vals[4]
    normed2, spread2 = normalize(hidden2)
    layer_out = (
        (normed2 * gain_vals[1] + bias_vals[5]).astype(jnp.bfloat16).reshape(count, length, width)
    )
    qkv_back, out_back, unused_bias, gain_back = fetch_attention()
    up_back, down_back, unused_up = fetch_ffn()
    gain_back = gain_back.astype(jnp.float32)
    grad_out = cotangent.reshape(rows, width).astype(jnp.float32)
    grad_h2 = norm_back(grad_out, gain_back[1], normed2, spread2)
    grad_f_low = grad_h2.astype(jnp.bfloat16).reshape(rows, GROUPS, group_w)
    down_grad = jnp.einsum(
        "lut,lux->utx",
        activ_low.reshape(rows, GROUPS, -1),
        grad_f_low,
        preferred_element_type=jnp.float32,
    ).reshape(-1, group_w)
    grad_act = jnp.einsum(
        "ipo,pso->ips",
        grad_f_low,
        down_back.reshape(GROUPS, -1, group_w),
        preferred_element_type=jnp.float32,
    ).reshape(rows, -1)
    grad_pre = gelu_pull(grad_act)[0].astype(jnp.bfloat16)
    up_bias_grad = jnp.sum(grad_pre, 0, dtype=jnp.float32)
    grad_pre_groups = grad_pre.reshape(rows, GROUPS, -1)
    up_grad = jnp.einsum(
        "ngc,ngf->gcf",
        layer1_low.reshape(rows, GROUPS, group_w),
        grad_pre_groups,
        preferred_element_type=jnp.float32,
    ).reshape(width, -1)
    grad_l1 = grad_h2 + jnp.einsum(
        "ngf,gcf->ngc",
        grad_pre_groups,
        up_back.reshape(GROUPS, group_w, -1),
        preferred_element_type=jnp.float32,
    ).reshape(rows, width)
    grad_h1 = norm_back(grad_l1, gain_back[0], normed1, spread1)
    grad_attn = grad_h1.astype(jnp.bfloat16)
    out_grad = jnp.einsum("nc,ne->ce", context, grad_attn, preferred_element_type=jnp.float32)
    grad_ctx = jnp.einsum(
        "ne,ce->nc", grad_attn, out_back, preferred_element_type=jnp.float32
    ).astype(jnp.bfloat16)
    grad_queries, grad_keys, grad_values = lax.map(
        attend_backward, (queries, keys_all, values_all, segment_ids, lse, grad_ctx.reshape(shape4))
    )
    grad_q = grad_queries.reshape(rows, width).astype(jnp.bfloat16)
    grad_k = grad_keys.reshape(rows, width).astype(jnp.bfloat16)
    grad_v = grad_values.reshape(rows, width).astype(jnp.bfloat16)
    grad_mixed = jnp.concatenate(
        [
            grad_q.reshape(rows, GROUPS, group_w),
            grad_k.reshape(rows, GROUPS, group_w),
            grad_v.reshape(rows, GROUPS, group_w),
        ],
        -1,
    )
    qkv_grad = jnp.einsum(
        "ngc,nge->gce",
        inputs.reshape(rows, GROUPS, group_w),
        grad_mixed,
        preferred_element_type=jnp.float32,
    ).reshape(width, -1)
    input_grad = grad_h1 + jnp.einsum(
        "nge,gce->ngc",
        grad_mixed,
        qkv_back.reshape(GROUPS, group_w, -1),
        preferred_element_type=jnp.float32,
    ).reshape(rows, width)
    bias_grad = jnp.stack(
        [
            jnp.sum(grad_q, 0, dtype=jnp.float32),
            jnp.sum(grad_v, 0, dtype=jnp.float32),
            jnp.sum(grad_h1, 0),
            jnp.sum(grad_l1, 0),
            jnp.sum(grad_h2, 0),
            jnp.sum(grad_out, 0),
        ]
    )
    gain_grad = jnp.stack([jnp.sum(grad_l1 * normed1, 0), jnp.sum(grad_out * normed2, 0)])
    qkv_sum, out_sum, bias_sum, gain_sum = (
        lax.psum_scatter(qkv_grad, ("dp", "fsdp"), scatter_dimension=0, tiled=True),
        lax.psum_scatter(out_grad, ("dp", "fsdp"), scatter_dimension=0, tiled=True),
        lax.psum_scatter(bias_grad, ("dp", "fsdp"), scatter_dimension=1, tiled=True),
        lax.psum_scatter(gain_grad, ("dp", "fsdp"), scatter_dimension=1, tiled=True),
    )
    ffn_sums = reduce_ffn(up_grad, down_grad, up_bias_grad)
    up_sum, down_sum, up_bias_sum = ffn_sums
    return (
        layer_out,
        input_grad.reshape(count, length, width),
        qkv_sum,
        out_sum,
        up_sum,
        down_sum,
        bias_sum,
        up_bias_sum,
        gain_sum,
    )


def solution(mesh):
    in_specs = (
        P(("dp", "fsdp"), None, None),
        P(("dp", "fsdp"), None),
        P(("dp", "fsdp"), None),
        P(("dp", "fsdp"), None),
        P(("dp", "fsdp"), None),
        P(("dp", "fsdp"), None),
        P(None, ("dp", "fsdp")),
        P(("dp", "fsdp")),
        P(None, ("dp", "fsdp")),
        P(("dp", "fsdp"), None, None),
    )
    out_specs = (
        P(("dp", "fsdp"), None, None),
        P(("dp", "fsdp"), None, None),
        P(("dp", "fsdp"), None),
        P(("dp", "fsdp"), None),
        P(("dp", "fsdp"), None),
        P(("dp", "fsdp"), None),
        P(None, ("dp", "fsdp")),
        P(("dp", "fsdp")),
        P(None, ("dp", "fsdp")),
    )
    return jax.shard_map(local, mesh=mesh, in_specs=in_specs, out_specs=out_specs, check_vma=False)
```

profile of v0, /device:TPU:0, one launch (start us, length us, event | category | flops | bytes accessed | tf_op | source)
XLA Modules:
  0.0 926.9 jit_solution(14447026839796752932)
XLA Ops:
  9.5 4.9 copy.94
  16.0 81.7 %all_gather.26 = bf16[768,576]{1,0:T(8,128)(2,1)} all-gather(bf16[24,576]{1,0:T(8,128)(2,1)S(1)} %copy-done.27), channel_id=1, replica_groups=mesh['dp'=4,'fsdp'=8] {'dp','fsdp'}, dimensions={0}, use_global_device_ids=true | all-gather | bytes 912384 | tf_op jit(solution)/shard_map/all_gather | solution.py:113
  97.7 3.8 reshape_reshape.4
  101.5 3.2 convolution_bitcast_fusion
  106.0 3.4 fusion.77
  109.6 37.1 %all-reduce = bf16[3072]{0:T(1024)(128)(2,1)S(1)} all-reduce(bf16[3072]{0:T(1024)(128)(2,1)S(1)} %dynamic-update-slice), channel_id=1, replica_groups=mesh['dp'=4,'fsdp'=8] {'dp','fsdp'}, use_global_device_ids=true, to_apply=%add | all-reduce | flops 3072 | bytes 12288
  146.7 65.6 %all-gather.1 = bf16[32,24,2]{1,2,0:T(2,128)(2,1)S(1)} all-gather(bf16[1,24,2]{1,2,0:T(2,128)(2,1)S(1)} %bitcast.304), channel_id=1, replica_groups=mesh['dp'=4,'fsdp'=8] {'dp','fsdp'}, dimensions={0}, use_global_device_ids=true | all-gather | bytes 3168 | tf_op jit(solution)/shard_map/all_gather | solution.py:116
  212.6 2.7 convert_reduce_fusion.3
  216.0 63.9 %all-gather = bf16[32,24,6]{1,2,0:T(8,128)(2,1)S(1)} all-gather(bf16[1,24,6]{1,2,0:T(8,128)(2,1)S(1)} %bitcast.303), channel_id=1, replica_groups=mesh['dp'=4,'fsdp'=8] {'dp','fsdp'}, dimensions={0}, use_global_device_ids=true | all-gather | bytes 9504 | tf_op jit(solution)/shard_map/all_gather | solution.py:115
  280.9 3.1 copy.125
  284.0 2.4 copy.121
  286.3 5.7 reshape.348
  292.0 2.3 convert_element_type.116
  294.4 1.7 copy.99
  296.1 5.7 reshape.347
  301.8 5.0 fusion.66
  308.1 21.2 %while.26 = (s32[]{:T(128)}, bf16[2,512,12,64]{1,3,2,0:T(8,128)(2,1)}, f32[2,12,512]{2,1,0:T(8,128)S(1)}, bf16[2,512,12,64]{1,3,2,0:T(8,128)(2,1)}, s32[2,512]{1...) while((s32[]{:T(128)}, ...), condition=%wide.region_3.4_spmd, body=%wide.region_0.3_spmd.sunk | while | flops 843836416 | bytes 42963044 | solution.py:149
  308.4 2.1 fusion.122
  310.5 2.6 fusion.123
  313.1 5.5 bitcast_dynamic-update-slice_fusion.10
  318.9 2.1 fusion.122
  321.0 2.6 fusion.123
  323.6 5.5 bitcast_dynamic-update-slice_fusion.10
  329.3 3.0 copy.100
  333.9 4.3 fusion.78
  341.6 33.3 %fusion.52 = (bf16[1024,4,768]{2,0,1:T(8,128)(2,1)}, f32[1024,4,768]{2,0,1:T(8,128)}, f32[4,1024,768]{2,1,0:T(8,128)}) fusion(f32[4,768]{1,0:T(4,128)S(1)} %reshape.363, bf16[1024,4,192]{0,2,1:T(8,128)(2,1)} %bitcast.281, bf16[4,192,768]{2,1,0:T(8,128)(2,1)} %bitcast.294), kind=kOutput, calls=%fused_computation.77 | convolution fusion | flops 1415577600 | bytes 34222080 | tf_op jit(solution)/shard_map/ngc,gce->nge/dot_general | solution.py:20
  374.9 5.6 fusion.79
  384.8 3.1 fusion.72
  390.5 15.7 %convert_reduce_fusion = (f32[4,768]{1,0:T(4,128)}, bf16[1024,4,768]{2,0,1:T(8,128)(2,1)}) fusion(f32[1024,4,768]{2,0,1:T(8,128)} %get-tuple-element.275, bf16[1024,4,192]{0,2,1:T(8,128)(2,1)S(1)} %bitcast.285, bf16[4,768,192]{2,1,0:T(8,128)(2,1)S(1)} %bitcast.293, f32[4,1024,768]{2,1,0:T(8,128)} %get-tuple-element.285, f32[4,768]{1,0:T(4,128)S(1)} %reshape.363), kind=kOutput, calls=%fused_computation.78 | convolution fusion | flops 1261433856 | bytes 34234368 | tf_op jit(solution)/shard_map/ipo,pso->ips/dot_general | solution.py:179
  406.2 5.1 fusion.80
  411.3 2.2 multiply_reduce_fusion.2
  413.6 1.7 fusion.73
  417.0 2.6 convolution_convert_fusion
  419.6 2.6 copy.107
  422.2 3.9 reshape.356
  426.0 2.9 copy.109
  433.0 49.2 %while.27 = (s32[]{:T(128)}, bf16[2,512,12,64]{1,3,2,0:T(8,128)(2,1)}, bf16[2,512,12,64]{1,3,2,0:T(8,128)(2,1)}, bf16[2,512,12,64]{1,3,2,0:T(8,128)(2,1)}, bf16[...) while((s32[]{:T(128)}, ...), condition=%wide.region_14.15_spmd, body=%wide.region_12.14_spmd.sunk | while | flops 2062019584 | bytes 143596848 | solution.py:206
  433.5 1.8 fusion.132
  435.4 3.9 bitcast_dynamic-update-slice_fusion.14
  439.3 6.9 multiply_reduce_fusion.10
  446.2 7.1 multiply_convert_fusion.2
  453.3 2.0 bitcast_dynamic-update-slice_fusion.13
  458.0 1.8 fusion.132
  459.9 3.9 bitcast_dynamic-update-slice_fusion.14
  463.8 6.9 multiply_reduce_fusion.10
  470.7 7.1 multiply_convert_fusion.2
  477.8 2.0 bitcast_dynamic-update-slice_fusion.13
  482.1 3.0 copy.111
  486.6 4.3 copy.112
  490.9 3.8 convert_element_type.135
  494.7 2.8 copy.110
  497.5 3.8 convert_element_type.131
  504.4 3.2 fusion.81
  507.7 6.7 fusion.84
  515.8 5.7 fusion.82
  521.7 5.2 fusion.69
  527.0 2.9 copy.124
  532.1 3.9 fusion.83
  536.8 2.4 copy.127
  539.2 39.6 %all-reduce.5 = (f32[6,768]{1,0:T(8,128)S(1)}, f32[3072]{0:T(1024)S(1)}, f32[2,768]{1,0:T(2,128)S(1)}) all-reduce(f32[6,768]{1,0:T(8,128)S(1)} %stack.36, f32[3072]{0:T(1024)S(1)} %reduce_sum.188, f32[2,768]{1,0:T(2,128)S(1)} %pad_maximum_fusion), channel_id=6, replica_groups=mesh['dp'=4,'fsdp'=8] {'dp','fsdp'}, use_global_device_ids=true, to_apply=%region_25.26.clone | all-reduce | flops 9216 | bytes 73728
  580.7 24.0 %reduce-scatter.17.cloned.1.call-done = f32[24,576]{1,0:T(8,128)} async-done(((f32[768,576]{1,0:T(8,128)}), f32[24,576]{1,0:T(8,128)}) %reduce-scatter.17.cloned.1.call-update) | async-done | bytes 55312
  604.7 106.4 %reduce-scatter.15.cloned.1.call-done = f32[96,192]{1,0:T(8,128)} async-done(((f32[3072,192]{1,0:T(8,128)}), f32[96,192]{1,0:T(8,128)}) %reduce-scatter.15.cloned.1.call-update) | async-done | bytes 73744
  711.1 103.7 %reduce-scatter.13.cloned.1.call-done = f32[24,768]{1,0:T(8,128)} async-done(((f32[768,768]{1,0:T(8,128)}), f32[24,768]{1,0:T(8,128)}) %reduce-scatter.13.cloned.1.call-update) | async-done | bytes 73744 | tf_op jit(solution)/shard_map/reduce_scatter | solution.py:92
  814.8 104.8 %reduce-scatter.11.cloned.1.call-done = f32[24,768]{1,0:T(8,128)} async-done(((f32[768,768]{1,0:T(8,128)}), f32[24,768]{1,0:T(8,128)}) %reduce-scatter.11.cloned.1.call-update) | async-done | bytes 73744 | tf_op jit(solution)/shard_map/reduce_scatter | solution.py:245
  (188 shorter events, 42.9 us)
Async XLA Ops:
  7.2 326.7 %all-gather.6.cloned.1.call-start = ((), (), s32[]{:S(2)}) async-start(), calls=%async_computation.4 | async-start | bytes 1216512 | tf_op jit(solution)/shard_map/all_gather | solution.py:114
  7.9 333.6 %all-gather.8.cloned.1.call-start = ((), (), s32[]{:S(2)}) async-start(), calls=%async_computation.5 | async-start | bytes 1216512 | tf_op jit(solution)/shard_map/all_gather | solution.py:121
  8.7 366.2 %all-gather.10.cloned.1.call-start = ((), (), s32[]{:S(2)}) async-start(), calls=%async_computation.6 | async-start | bytes 1622016 | tf_op jit(solution)/shard_map/all_gather | solution.py:122
  9.4 595.3 %reduce-scatter.17.cloned.1.call-start = ((), (), s32[]{:S(2)}) async-start(), calls=%async_computation.10 | async-start | bytes 2027520
  14.4 1.7 copy-start.27
  106.0 3.4 copy-start.41
  106.0 40.7 %copy-start.39 = (bf16[2,24]{1,0:T(2,128)(2,1)S(1)}, bf16[2,24]{1,0:T(2,128)(2,1)}, u32[]{:S(2)}) copy-start(bf16[2,24]{1,0:T(2,128)(2,1)} %param.22) | copy-start | bytes 292
  106.0 109.9 %copy-start.38 = (bf16[6,24]{1,0:T(8,128)(2,1)S(1)}, bf16[6,24]{1,0:T(8,128)(2,1)}, u32[]{:S(2)}) copy-start(bf16[6,24]{1,0:T(8,128)(2,1)} %param.20) | copy-start | bytes 868
  212.6 3.3 copy-start.25
  286.3 5.7 copy-start.16
  301.8 6.3 copy-start.24
  338.3 1.6 copy-start
  374.9 5.6 copy-start.1
  374.9 5.6 copy-start.35
  381.3 1.9 copy-start.2
  381.3 1.9 copy-start.26
  383.2 1.6 copy-start.33
  383.2 1.6 copy-start.34
  387.9 1.7 copy-start.3
  387.9 2.5 copy-start.22
  389.8 16.4 %copy-start.20 = (bf16[1024,768]{0,1:T(8,128)(2,1)}, bf16[1024,768]{0,1:T(8,128)(2,1)S(1)}, u32[]{:S(2)}) copy-start(bf16[1024,768]{0,1:T(8,128)(2,1)S(1)} %convert_element_type.126) | copy-start | bytes 4718596
  390.5 15.7 %copy-start.23 = (bf16[768,768]{1,0:T(8,128)(2,1)S(1)}, bf16[768,768]{1,0:T(8,128)(2,1)}, u32[]{:S(2)}) copy-start(bf16[768,768]{1,0:T(8,128)(2,1)} %all-gather.8.cloned.1.call-done) | copy-start | bytes 3538948
  406.2 5.1 copy-start.4
  413.6 3.4 copy-start.40
  415.3 1.7 copy-start.10
  433.5 1.9 copy-start.6
  435.4 4.0 copy-start.5
  446.2 7.1 copy-start.17
  453.3 2.0 copy-start.7
  455.4 1.2 copy-start.18
  456.5 1.1 copy-start.8
  458.0 1.9 copy-start.6
  459.9 4.0 copy-start.5
  470.7 7.1 copy-start.17
  477.8 2.0 copy-start.7
  479.8 1.2 copy-start.18
  481.0 1.1 copy-start.8
  486.6 8.1 copy-start.9
  501.3 1.9 copy-start.19
  502.9 1.5 copy-start.13
  504.4 3.2 copy-start.14
  504.4 3.3 copy-start.21
  507.6 203.5 %reduce-scatter.15.cloned.1.call-start = ((), (), s32[]{:S(2)}) async-start(), calls=%async_computation.9 | async-start | bytes 3244032
  514.4 1.4 copy-start.15
  514.4 300.3 %reduce-scatter.13.cloned.1.call-start = ((), (), s32[]{:S(2)}) async-start(), calls=%async_computation.8 | async-start | bytes 2433024 | tf_op jit(solution)/shard_map/reduce_scatter | solution.py:92
  521.6 5.3 copy-start.30
  521.6 5.4 copy-start.36
  521.6 5.4 copy-start.31
  521.6 397.9 %reduce-scatter.11.cloned.1.call-start = ((), (), s32[]{:S(2)}) async-start(), calls=%async_computation.7 | async-start | bytes 2433024 | tf_op jit(solution)/shard_map/reduce_scatter | solution.py:245
  526.9 3.0 copy-start.37
  526.9 3.0 copy-start.29
  526.9 3.0 copy-start.28
  526.9 3.1 copy-start.32
  527.0 5.1 copy-start.12
  532.1 3.9 copy-start.11
Sparse Core Ops, SparseCore 0:
  10.9 57.2 all-gather.5
  71.1 53.4 all-gather.7
  127.5 53.8 all-gather.9
  507.8 96.8 reduce-scatter.16
  610.5 100.5 reduce-scatter.14
  716.8 97.9 reduce-scatter.12
  821.5 98.0 reduce-scatter.10
where the time goes:
time: 933 us; the launch traced here: 927 us
  waiting for transfers between devices  341 us (37%)
  blocking collectives  288 us (31%)
  matrix products  141 us (15%)
  local copies, waits for them, and re-layouts  95.8 us (10%)
  other arithmetic  44.8 us (5%)
  between operations  15.1 us (2%)
    unnamed x9, waiting for transfers between devices  133 us
    reduce_scatter x1, waiting for transfers between devices, local(): lax.psum_scatter(out_grad, ('dp', 'fsdp'), scatter_dimension=0, tiled=True)  105 us
    reduce_scatter x1, waiting for transfers between devices, reduce_ffn(): lax.psum_scatter(up_grad, ('dp', 'fsdp'), scatter_dimension=0, tiled=True)  104 us
    all_gather x1, blocking collectives, fetch_attention(): lax.all_gather(qkv_weight, ('dp', 'fsdp'), axis=0, tiled=True)  81.7 us
    unnamed x2, blocking collectives  76.7 us
    all_gather x1, blocking collectives, fetch_attention(): lax.all_gather(gains, ('dp', 'fsdp'), axis=1, tiled=True)  65.6 us
    all_gather x1, blocking collectives, fetch_attention(): lax.all_gather(biases, ('dp', 'fsdp'), axis=1, tiled=True)  63.9 us
    dot_general x3, matrix products, group_apply(): jnp.einsum('ngc,gce->nge', parts, table, preferred_element_type=jnp.float32)  42 us
  transfers between devices with their start and end apart: 7, of which 4 were waited for; matrix products, arithmetic and copies ran while one was open for 16% of the time, Pallas kernels for 0%

commit v1 on v0

v1 whole, which is shorter than its diff:
```python
from functools import partial

import jax
import jax.numpy as jnp
from jax import lax
from jax.experimental import pallas as pl
from jax.experimental.pallas import tpu as pltpu
from jax.sharding import PartitionSpec as P

HEADS = 12
GROUPS = 4
EPSILON = 1e-05
SCORE_SCALE = 0.125
FAR = -1e30
F32 = jnp.float32
BF16 = jnp.bfloat16
ERF_P = 0.39
ERF_C = (
    0.23532515472880694, 0.09138881837358971, 0.6495583919191722,
    -0.6353990321145604, 0.8866636029850097, -0.22753693758818713,
)
NT = (((1,), (1,)), ((), ()))
TN = (((0,), (0,)), ((), ()))


def dot(a, b):
    return jnp.dot(a, b, preferred_element_type=F32)


def dot_nt(a, b):
    return lax.dot_general(a, b, NT, preferred_element_type=F32)


def dot_tn(a, b):
    return lax.dot_general(a, b, TN, preferred_element_type=F32)


def edge(group):
    return (group // 2) * 384 + (group % 2) * 128


def inset(group):
    return (group % 2) * 64


def aligned(value, step):
    return value if isinstance(value, int) else pl.multiple_of(value, step)


def lane_ids(shape):
    return lax.broadcasted_iota(jnp.int32, shape, len(shape) - 1)


def head_only(block, head, extra=False):
    lanes = lane_ids(block.shape)
    keep = (lanes >= 64 * head) & (lanes < 64 * head + 64)
    if extra:
        keep = keep | (lanes >= 192)
    return jnp.where(keep, block, jnp.zeros_like(block))


def gelu_pair(v):
    a = jnp.abs(v)
    u = jnp.exp(v * v * (-0.5))
    t = 1.0 / (1.0 + a * (ERF_P * 0.7071067811865476))
    h = ERF_C[5] * 0.5
    for c in ERF_C[4::-1]:
        h = h * t + 0.5 * c
    h = h * t * u
    phi = jnp.where(v >= 0, 1.0 - h, h)
    return v * phi, phi + v * u * 0.3989422804014327


def normalize(hidden):
    centre = hidden - jnp.mean(hidden, -1, keepdims=True)
    spread = lax.rsqrt(jnp.mean(centre * centre, -1, keepdims=True) + EPSILON)
    return centre * spread, spread


def norm_back(upstream, gain, normed, spread):
    scaled = upstream * gain
    return spread * (
        scaled
        - jnp.mean(scaled, -1, keepdims=True)
        - normed * jnp.mean(scaled * normed, -1, keepdims=True)
    )


def spread_windows(parts):
    tiles = []
    for pair in range(2):
        low, high = parts[2 * pair], parts[2 * pair + 1]
        tiles += [low[:, :128], low[:, 128:] + high[:, :128], high[:, 128:]]
    return jnp.concatenate(tiles, -1)


def col_sum(v):
    return jnp.sum(v, 0, keepdims=True)


def body(
    x_ref, seg_ref, cot_ref, buf_a, buf_o, buf_u, buf_d,
    lo_ref, ig_ref, ga_ref, go_ref, gu_ref, gd_ref,
    piece, wqkv, wo, wup, wdn, small, rows_sm, upb,
    qext, kext, qs, kk, vv, ctx, gctx, gm, lse, lse_t,
    acc_o, acc_u, acc_d, acc_q, acc_b, acc_ub, acc_qv, tmp_t,
):
    count, length = seg_ref.shape
    rows, width = x_ref.shape
    n_dev, take, _ = buf_a.shape
    per = n_dev // GROUPS
    take_d = buf_d.shape[1]

    wqkv[...] = jnp.zeros_like(wqkv)
    wo[...] = jnp.zeros_like(wo)
    wup[...] = jnp.zeros_like(wup)
    wdn[...] = jnp.zeros_like(wdn)
    acc_q[...] = jnp.zeros_like(acc_q)
    acc_o[...] = jnp.zeros_like(acc_o)
    acc_u[...] = jnp.zeros_like(acc_u)
    acc_d[...] = jnp.zeros_like(acc_d)
    acc_b[...] = jnp.zeros_like(acc_b)
    acc_ub[...] = jnp.zeros_like(acc_ub)
    acc_qv[...] = jnp.zeros_like(acc_qv)
    lse[...] = jnp.zeros_like(lse)

    for b in range(count):
        seg = seg_ref[b : b + 1, :]
        doc = lax.broadcasted_iota(jnp.int32, (128, length), 0) - 64
        k_t = jnp.where((doc >= 0) & (seg == doc), 1.0, 0.0).astype(F32)
        q_t = jnp.where(
            (doc == 0) | ((doc > 0) & (seg != doc) & (seg != 0)), FAR, 0.0
        ).astype(F32)
        here = pl.ds(b * length, length)
        kext[here, :] = k_t.T.astype(BF16)
        qext[here, :] = q_t.T.astype(BF16)

    def gather(buf, group, cols, step):
        align = 8 if step % 8 == 0 else 1

        def one(p, _):
            at = pl.multiple_of(p * step, align)
            piece[pl.ds(at, step), 0:cols] = buf[group * per + p].astype(F32)
            return 0

        lax.fori_loop(0, per, one, 0)

    def take_qkv(g, _):
        gather(buf_a, g, 640, take)
        where = pl.ds(pl.multiple_of(inset(g), 64), 192)
        for part in range(3):
            wqkv[g, where, 256 * part : 256 * part + 192] = piece[
                0:192, 192 * part : 192 * part + 192
            ].astype(BF16)
        small[g] = piece[0:192, 512:640].T[64:80]
        return 0

    lax.fori_loop(0, GROUPS, take_qkv, 0)

    def take_rest(g, _):
        where = pl.ds(pl.multiple_of(inset(g), 64), 192)
        gather(buf_o, g, 768, take)
        wo[g, 0:192, :] = piece[0:192, 0:768].astype(BF16)
        gather(buf_u, g, 768, take)
        wup[g, where, :] = piece[0:192, 0:768].astype(BF16)
        gather(buf_d, g, 256, take_d)
        upb[g] = piece[0:768, 128:256].T[64:72]
        w = piece[0:768, 0:192].astype(BF16)

        @pl.when(g % 2 == 0)
        def _():
            wdn[g, :, 0:192] = w

        @pl.when(g % 2 == 1)
        def _():
            wdn[g, :, 64:256] = w

        return 0

    lax.fori_loop(0, GROUPS, take_rest, 0)
    rows_sm[...] = jnp.concatenate([small[g] for g in range(GROUPS)], -1)

    pad64 = jnp.zeros((1, 64), F32)

    def attend(g, b):
        here = pl.ds(pl.multiple_of(b * length, length), length)
        xw = x_ref[here, pl.ds(pl.multiple_of(edge(g), 128), 256)]
        bias = small[g]
        bq = jnp.concatenate([bias[0:1], pad64], -1)
        bv = jnp.concatenate([bias[1:2], pad64], -1)
        q = (dot(xw, wqkv[g, :, 0:256]) + bq).astype(BF16) * BF16(SCORE_SCALE)
        k = dot(xw, wqkv[g, :, 256:512]).astype(BF16)
        v = (dot(xw, wqkv[g, :, 512:768]) + bv).astype(BF16)
        qs[g, here, 0:128] = q[:, :128]
        qs[g, here, 128:256] = q[:, 128:] + qext[here, :]
        kk[g, here, 0:128] = k[:, :128]
        kk[g, here, 128:256] = k[:, 128:] + kext[here, :]
        vv[g, here, :] = v
        q = qs[g, here, :]
        k = kk[g, here, :]
        lanes = lane_ids((length, 128))
        out = jnp.zeros((length, 256), F32)
        for h in range(3):
            s = dot_nt(head_only(q, h, True), k)
            top = jnp.max(s, -1, keepdims=True)
            e = jnp.exp(s - top)
            total = jnp.sum(e, -1, keepdims=True)
            p = (e * (1.0 / total)).astype(BF16)
            out = out + dot(p, head_only(v, h))
            lse[here, :] = jnp.where(lanes == 3 * g + h, top + jnp.log(total), lse[here, :])
        ctx[g, here, :] = out.astype(BF16)

    def attend_step(i, _):
        attend(i // count, i % count)
        return 0

    lax.fori_loop(0, GROUPS * count, attend_step, 0)
    lse_t[...] = lse[...].T

    block = 256

    def ffn(i, _):
        here = pl.ds(pl.multiple_of(i * block, block), block)
        small_rows = rows_sm[...]
        b_out, b_n1, b_ff, b_n2 = (small_rows[j : j + 1] for j in (2, 3, 4, 5))
        gain1, gain2 = small_rows[6:7], small_rows[7:8]
        attn = dot(ctx[0, here, :], wo[0])
        for g in range(1, GROUPS):
            attn = attn + dot(ctx[g, here, :], wo[g])
        hidden1 = x_ref[here, :].astype(F32) + attn + b_out
        normed1, spread1 = normalize(hidden1)
        layer1 = normed1 * gain1 + b_n1
        low1 = layer1.astype(BF16)
        acts, slopes, outs = [], [], []
        for g in range(GROUPS):
            pre = dot(low1[:, edge(g) : edge(g) + 256], wup[g]) + upb[g, 0:1, :]
            act, slope = gelu_pair(pre)
            act = act.astype(BF16)
            acts.append(act)
            slopes.append(slope)
            outs.append(dot(act, wdn[g]))
        hidden2 = layer1 + spread_windows(outs) + b_ff
        normed2, spread2 = normalize(hidden2)
        lo_ref[here, :] = (normed2 * gain2 + b_n2).astype(BF16)
        cot = cot_ref[here, :].astype(F32)
        grad_h2 = norm_back(cot, gain2, normed2, spread2)
        low_f = grad_h2.astype(BF16)
        f_t = low_f.T
        l_t = low1.T
        backs = []
        for g in range(GROUPS):
            acc_d[g] += dot(f_t[192 * g : 192 * g + 192], acts[g])
            grad_act = dot_nt(low_f[:, edge(g) : edge(g) + 256], wdn[g])
            grad_pre = (grad_act * slopes[g]).astype(BF16)
            acc_ub[g, 0:1, :] += col_sum(grad_pre.astype(F32))
            acc_u[g] += dot(l_t[192 * g : 192 * g + 192], grad_pre)
            backs.append(dot_nt(grad_pre, wup[g]))
        grad_l1 = grad_h2 + spread_windows(backs)
        grad_h1 = norm_back(grad_l1, gain1, normed1, spread1)
        ig_ref[here, :] = grad_h1
        low_a = grad_h1.astype(BF16)
        for g in range(GROUPS):
            gctx[g, here, :] = dot_nt(low_a, wo[g]).astype(BF16)
            acc_o[g] += dot(ctx[g, here, :].T[0:192], low_a)
        acc_b[2:3] += col_sum(grad_h1)
        acc_b[3:4] += col_sum(grad_l1)
        acc_b[4:5] += col_sum(grad_h2)
        acc_b[5:6] += col_sum(cot)
        acc_b[6:7] += col_sum(grad_l1 * normed1)
        acc_b[7:8] += col_sum(cot * normed2)
        return 0

    lax.fori_loop(0, rows // block, ffn, 0)

    def attend_back(g, b):
        here = pl.ds(pl.multiple_of(b * length, length), length)
        q = qs[g, here, :]
        k = kk[g, here, :]
        v = vv[g, here, :]
        d_out = gctx[g, here, :]
        d_q = jnp.zeros((length, 256), F32)
        d_k = jnp.zeros((length, 256), F32)
        d_v = jnp.zeros((length, 256), F32)
        for h in range(3):
            s_t = dot_nt(k, head_only(q, h, True))
            p_t = jnp.exp(s_t - lse_t[pl.ds(3 * g + h, 1), here])
            d_h = head_only(d_out, h)
            dp_t = dot_nt(v, d_h)
            inner = col_sum(p_t * dp_t)
            ds_t = (p_t * (dp_t - inner)).astype(BF16)
            d_v = d_v + dot(p_t.astype(BF16), d_h)
            d_k = d_k + dot(ds_t, head_only(q, h))
            d_q = d_q + dot_tn(ds_t, head_only(k, h))
        low_q = (d_q * SCORE_SCALE).astype(BF16)
        low_v = d_v.astype(BF16)
        gm[here, 0:256] = low_q
        gm[here, 256:512] = d_k.astype(BF16)
        gm[here, 512:768] = low_v
        acc_qv[g, 0:1, :] += col_sum(low_q.astype(F32))
        acc_qv[g, 1:2, :] += col_sum(low_v.astype(F32))

    def back_step(g, _):
        for b in range(count):
            attend_back(g, b)
        mixed = gm[...]
        at = pl.ds(pl.multiple_of(edge(g), 128), 256)
        xw = x_ref[:, at]
        tmp_t[...] = dot(xw.T, mixed)
        acc_q[g] = tmp_t[pl.ds(pl.multiple_of(inset(g), 64), 192), :]
        ig_ref[:, at] += dot_nt(mixed, wqkv[g])
        return 0

    lax.fori_loop(0, GROUPS, back_step, 0)

    def scatter(buf, group, cols, step):
        align = 8 if step % 8 == 0 else 1

        def one(p, _):
            at = pl.multiple_of(p * step, align)
            buf[group * per + p] = piece[pl.ds(at, step), 0:cols].astype(buf.dtype)
            return 0

        lax.fori_loop(0, per, one, 0)

    for g in range(GROUPS):
        for part in range(3):
            piece[0:192, 192 * part : 192 * part + 192] = acc_q[g, :, 256 * part : 256 * part + 192]
        mine = jnp.concatenate(
            [acc_qv[g, 0:2, 0:192], acc_b[2:8, 192 * g : 192 * g + 192]], 0
        )
        high = mine.astype(BF16).astype(F32)
        side = jnp.concatenate([high, mine - high, jnp.zeros((112, 192), F32)], 0)
        piece[0:192, 576:640] = side.T[:, 0:64]
        scatter(ga_ref, g, 640, take)
        piece[0:192, 0:768] = acc_o[g]
        scatter(go_ref, g, 768, take)
        piece[0:192, 0:768] = acc_u[g]
        scatter(gu_ref, g, 768, take)
        ub = acc_ub[g, 0:1, :]
        high = ub.astype(BF16).astype(F32)
        full = jnp.concatenate([acc_d[g], high, ub - high, jnp.zeros((62, 768), F32)], 0)
        piece[0:768, 0:256] = full.T
        scatter(gd_ref, g, 256, take_d)


def layer(tokens, segment_ids, cotangent, buf_a, buf_o, buf_u, buf_d):
    count, length, width = tokens.shape
    rows = count * length
    grad = lambda buf: jax.ShapeDtypeStruct(buf.shape, BF16)
    scratch = [
        pltpu.VMEM((768, 768), F32),
        pltpu.VMEM((4, 256, 768), BF16),
        pltpu.VMEM((4, 256, 768), BF16),
        pltpu.VMEM((4, 256, 768), BF16),
        pltpu.VMEM((4, 768, 256), BF16),
        pltpu.VMEM((4, 16, 192), F32),
        pltpu.VMEM((16, 768), F32),
        pltpu.VMEM((4, 8, 768), F32),
        pltpu.VMEM((rows, 128), BF16),
        pltpu.VMEM((rows, 128), BF16),
        pltpu.VMEM((4, rows, 256), BF16),
        pltpu.VMEM((4, rows, 256), BF16),
        pltpu.VMEM((4, rows, 256), BF16),
        pltpu.VMEM((4, rows, 256), BF16),
        pltpu.VMEM((4, rows, 256), BF16),
        pltpu.VMEM((rows, 768), BF16),
        pltpu.VMEM((rows, 128), F32),
        pltpu.VMEM((128, rows), F32),
        pltpu.VMEM((4, 192, 768), F32),
        pltpu.VMEM((4, 192, 768), F32),
        pltpu.VMEM((4, 192, 768), F32),
        pltpu.VMEM((4, 192, 768), F32),
        pltpu.VMEM((8, 768), F32),
        pltpu.VMEM((4, 8, 768), F32),
        pltpu.VMEM((4, 8, 256), F32),
        pltpu.VMEM((256, 768), F32),
    ]
    vm = pl.BlockSpec(memory_space=pltpu.VMEM)
    return pl.pallas_call(
        body,
        out_shape=(
            jax.ShapeDtypeStruct((rows, width), BF16),
            jax.ShapeDtypeStruct((rows, width), F32),
            grad(buf_a), grad(buf_o), grad(buf_u), grad(buf_d),
        ),
        in_specs=[vm] * 7,
        out_specs=[vm] * 6,
        scratch_shapes=scratch,
        compiler_params=pltpu.CompilerParams(vmem_limit_bytes=62 * 1024 * 1024),
    )(tokens.reshape(rows, width), segment_ids, cotangent.reshape(rows, width), buf_a, buf_o, buf_u, buf_d)


def local(tokens, segment_ids, qkv_weight, out_weight, up_weight, down_weight, biases, up_bias, gains, cotangent):
    axes = ("dp", "fsdp")
    take, take_d = qkv_weight.shape[0], down_weight.shape[0]
    zeros = lambda r, c: jnp.zeros((r, c), BF16)
    pack_a = jnp.concatenate([qkv_weight, biases.T, gains.T, zeros(take, 56)], 1)
    pack_d = jnp.concatenate([down_weight, up_bias[:, None], zeros(take_d, 63)], 1)
    gather = lambda v: lax.all_gather(v, axes, axis=0, tiled=True).reshape(32, -1, v.shape[1])
    out, ig, ga, go, gu, gd = layer(
        tokens, segment_ids, cotangent, gather(pack_a), gather(out_weight), gather(up_weight), gather(pack_d)
    )
    total = lambda v: lax.psum_scatter(
        v.reshape(-1, v.shape[2]).astype(F32), axes, scatter_dimension=0, tiled=True
    )
    ga, go, gu, gd = total(ga), total(go), total(gu), total(gd)
    side = (ga[:, 576:584] + ga[:, 584:592]).T
    return (
        out.reshape(tokens.shape), ig.reshape(tokens.shape),
        ga[:, :576], go, gu, gd[:, :192], side[:6], gd[:, 192] + gd[:, 193], side[6:8],
    )


def solution(mesh):
    row, col = P(("dp", "fsdp")), P(None, ("dp", "fsdp"))
    in_specs = (row, row, row, row, row, row, col, row, col, row)
    out_specs = (row, row, row, row, row, row, col, row, col)
    return jax.shard_map(local, mesh=mesh, in_specs=in_specs, out_specs=out_specs, check_vma=False)
```

time: 933 us -> 727 us (0.78)
  blocking collectives: 288 us -> 80.9 us
  waiting for transfers between devices: 341 us -> 522 us
  matrix products: 141 us -> 0 us
  Pallas kernels: 0 us -> 86.7 us
  local copies, waits for them, and re-layouts: 95.8 us -> 10.7 us
  other arithmetic: 44.8 us -> 11.5 us
    dot_general x25 -> x0, matrix products: 135 us -> none  [the longest x3 42 us: group_apply(): jnp.einsum('ngc,gce->nge', parts, table, preferred_element_type=jnp.float32)]
    all_gather x3 -> x1, blocking collectives: 211 us -> 80.9 us  [local(): lax.all_gather(v, axes, axis=0, tiled=True).reshape(32, -1, v.shape[1])]
    reduce_scatter x2 -> x3, waiting for transfers between devices: 208 us -> 310 us  [local(): lax.psum_scatter(v.reshape(-1, v.shape[2]).astype(F32), axes, scatter_dim...]
    all_gather x3, waiting for transfers between devices: 0.02 us -> 88.2 us  [local(): lax.all_gather(v, axes, axis=0, tiled=True).reshape(32, -1, v.shape[1])]
    pallas_call x0 -> x1, Pallas kernels: none -> 86.7 us  [layer(): pl.pallas_call(body, out_shape=(jax.ShapeDtypeStruct((rows, width), BF16)...]
    unnamed x2 -> x0, blocking collectives: 76.7 us -> none
    convert_element_type x15 -> x1, local copies, waits for them, and re-layouts: 32.9 us -> 1.86 us  [local(): v.reshape(-1, v.shape[2]).astype(F32)]
    unnamed x84 -> x9, local copies, waits for them, and re-layouts: 25.5 us -> 4.63 us
  transfers between devices with their start and end apart: 7 -> 7, of which waited for: 4 -> 6; matrix products, arithmetic and copies ran while one was open for 16% -> 2% of each run, Pallas kernels for 0% -> 0%
where the time goes in v1:
time: 727 us; the launch traced here: 726 us
  waiting for transfers between devices  522 us (72%)
  Pallas kernels  86.7 us (12%)
  blocking collectives  80.9 us (11%)
  between operations  14.2 us (2%)
  other arithmetic  11.5 us (2%)
  local copies, waits for them, and re-layouts  10.7 us (1%)
    reduce_scatter x3, waiting for transfers between devices, local(): lax.psum_scatter(v.reshape(-1, v.shape[2]).astype(F32), axes, scatter_dim...  310 us
    unnamed x8, waiting for transfers between devices  124 us
    all_gather x3, waiting for transfers between devices, local(): lax.all_gather(v, axes, axis=0, tiled=True).reshape(32, -1, v.shape[1])  88.2 us
    pallas_call x1, Pallas kernels, layer(): pl.pallas_call(body, out_shape=(jax.ShapeDtypeStruct((rows, width), BF16)...  86.7 us
    all_gather x1, blocking collectives, local(): lax.all_gather(v, axes, axis=0, tiled=True).reshape(32, -1, v.shape[1])  80.9 us
  transfers between devices with their start and end apart: 7, of which 6 were waited for; matrix products, arithmetic and copies ran while one was open for 2% of the time, Pallas kernels for 0%

profile of v1, /device:TPU:0, one launch (start us, length us, event | category | flops | bytes accessed | tf_op | source)
XLA Modules:
  0.0 726.5 jit_solution(13090617697986268803)
XLA Ops:
  7.2 0.0 all-gather.4.cloned.1.call-start
  7.2 0.7 all-gather.4.cloned.1.call-update
  7.9 0.0 all-gather.6.cloned.1.call-start
  8.0 0.7 all-gather.6.cloned.1.call-update
  8.7 0.0 all-gather.8.cloned.1.call-start
  8.7 0.8 copy.31
  9.5 0.1 pad.2.clone
  9.6 1.5 maximum_maximum_fusion
  11.1 0.0 all-gather.8.cloned.1.call-update
  11.1 0.0 all-reduce.3.cloned.1.call-start
  11.1 0.8 copy.29
  11.9 0.7 copy.30
  12.7 0.1 pad.6.clone
  12.7 0.8 maximum_maximum_fusion.1
  13.6 80.9 %all_gather.12 = bf16[768,640]{1,0:T(8,128)(2,1)} all-gather(bf16[24,640]{1,0:T(8,128)(2,1)S(1)} %maximum_maximum_fusion.1), channel_id=1, replica_groups=mesh['dp'=4,'fsdp'=8] {'dp','fsdp'}, dimensions={0}, use_global_device_ids=true | all-gather | bytes 1013760 | tf_op jit(solution)/shard_map/all_gather | solution.py:399
  94.5 0.0 all-gather.4.cloned.1.call-done
  94.5 30.7 %all-gather.6.cloned.1.call-done = bf16[768,768]{1,0:T(8,128)(2,1)} async-done(((bf16[24,768]{1,0:T(8,128)(2,1)}), bf16[768,768]{1,0:T(8,128)(2,1)}) %all-gather.6.cloned.1.call-update) | async-done | bytes 1179664 | tf_op jit(solution)/shard_map/all_gather | solution.py:399
  125.2 57.5 %all-gather.8.cloned.1.call-done = bf16[3072,256]{1,0:T(8,128)(2,1)} async-done(((bf16[96,256]{1,0:T(8,128)(2,1)}), bf16[3072,256]{1,0:T(8,128)(2,1)}) %all-gather.8.cloned.1.call-update) | async-done | bytes 1572880 | tf_op jit(solution)/shard_map/all_gather | solution.py:399
  182.7 86.7 %shard_map.169 = (bf16[1024,768]{1,0:T(8,128)(2,1)}, f32[1024,768]{1,0:T(8,128)}, bf16[32,24,640]{2,1,0:T(8,128)(2,1)}, bf16[32,24,768]{2,1,0:T(8,128)(2,1)}, bf...) custom-call(bf16[1024,768]{1,0:T(8,128)(2,1)} %bitcast.30, s32[2,512]{1,0:T(2,128)} %seg_ref.1, ...), custom_call_target="tpu_custom_call" | custom-call | tf_op jit(solution)/shard_map/pallas_call | solution.py:379
  269.4 1.3 bitcast_convert_fusion.3
  270.7 1.9 copy.32
  272.6 0.0 copy-start
  272.6 0.0 all-reduce.3.cloned.1.call-update
  272.6 0.0 reduce-scatter.9.cloned.1.call-start
  272.6 1.3 copy-done
  274.0 2.0 bitcast_convert_fusion
  275.9 0.0 copy-start.2
  275.9 0.0 reduce-scatter.9.cloned.1.call-update
  276.0 0.0 reduce-scatter.5.cloned.1.call-start
  276.0 1.3 copy-done.2
  277.3 1.7 bitcast_convert_fusion.2
  279.1 0.0 copy-start.1
  279.1 0.0 reduce-scatter.5.cloned.1.call-update
  279.1 0.0 reduce-scatter.7.cloned.1.call-start
  279.1 1.2 copy-done.1
  280.3 1.7 bitcast_convert_fusion.1
  282.0 0.0 reduce-scatter.7.cloned.1.call-update
  282.0 122.9 %all-reduce.3.cloned.1.call-done = f32[768,640]{0,1:T(8,128)} async-done(((f32[768,640]{0,1:T(8,128)}), f32[768,640]{0,1:T(8,128)}) %all-reduce.3.cloned.1.call-update) | async-done | bytes 1966096
  404.9 0.9 fusion.1
  405.8 0.0 copy-start.3
  405.8 0.6 slice.31
  406.4 1.2 constant_dynamic-slice_fusion
  407.6 0.8 copy.33
  408.3 102.7 %reduce-scatter.9.cloned.1.call-done = f32[96,256]{1,0:T(8,128)} async-done(((f32[3072,256]{1,0:T(8,128)}), f32[96,256]{1,0:T(8,128)}) %reduce-scatter.9.cloned.1.call-update) | async-done | bytes 98320 | tf_op jit(solution)/shard_map/reduce_scatter | solution.py:403
  511.1 1.6 fusion
  512.7 102.1 %reduce-scatter.5.cloned.1.call-done = f32[24,768]{1,0:T(8,128)} async-done(((f32[768,768]{1,0:T(8,128)}), f32[24,768]{1,0:T(8,128)}) %reduce-scatter.5.cloned.1.call-update) | async-done | bytes 73744 | tf_op jit(solution)/shard_map/reduce_scatter | solution.py:403
  614.8 104.8 %reduce-scatter.7.cloned.1.call-done = f32[24,768]{1,0:T(8,128)} async-done(((f32[768,768]{1,0:T(8,128)}), f32[24,768]{1,0:T(8,128)}) %reduce-scatter.7.cloned.1.call-update) | async-done | bytes 73744 | tf_op jit(solution)/shard_map/reduce_scatter | solution.py:403
  719.6 0.0 copy-done.3
  (2 shorter events, 0.0 us)
Async XLA Ops:
  7.2 87.3 %all-gather.4.cloned.1.call-start = ((), (), s32[]{:S(2)}) async-start(), calls=%async_computation.3 | async-start | bytes 1216512 | tf_op jit(solution)/shard_map/all_gather | solution.py:399
  7.9 117.3 %all-gather.6.cloned.1.call-start = ((), (), s32[]{:S(2)}) async-start(), calls=%async_computation.4 | async-start | bytes 1216512 | tf_op jit(solution)/shard_map/all_gather | solution.py:399
  8.7 174.0 %all-gather.8.cloned.1.call-start = ((), (), s32[]{:S(2)}) async-start(), calls=%async_computation.5 | async-start | bytes 1622016 | tf_op jit(solution)/shard_map/all_gather | solution.py:399
  11.1 393.9 %all-reduce.3.cloned.1.call-start = ((), (), s32[]{:S(2)}) async-start(), calls=%async_computation.9 | async-start | bytes 3932160
  272.6 1.4 copy-start
  272.6 238.5 %reduce-scatter.9.cloned.1.call-start = ((), (), s32[]{:S(2)}) async-start(), calls=%async_computation.8 | async-start | bytes 3244032 | tf_op jit(solution)/shard_map/reduce_scatter | solution.py:403
  275.9 1.4 copy-start.2
  276.0 338.8 %reduce-scatter.5.cloned.1.call-start = ((), (), s32[]{:S(2)}) async-start(), calls=%async_computation.6 | async-start | bytes 2433024 | tf_op jit(solution)/shard_map/reduce_scatter | solution.py:403
  279.1 1.3 copy-start.1
  279.1 440.5 %reduce-scatter.7.cloned.1.call-start = ((), (), s32[]{:S(2)}) async-start(), calls=%async_computation.7 | async-start | bytes 2433024 | tf_op jit(solution)/shard_map/reduce_scatter | solution.py:403
  405.8 313.8 %copy-start.3 = (f32[8,24]{1,0:T(8,128)}, f32[8,24]{1,0:T(8,128)S(1)}, u32[]{:S(2)}) copy-start(f32[8,24]{1,0:T(8,128)S(1)} %fusion.1) | copy-start | bytes 2308
Sparse Core Ops, SparseCore 0:
  10.9 57.3 all-gather.3
  71.2 53.9 all-gather.5
  128.7 53.9 all-gather.7
  272.7 132.1 all-reduce.2
  410.8 100.2 reduce-scatter.8
  516.8 97.9 reduce-scatter.4
  621.5 98.0 reduce-scatter.6

commit v2 on v1

--- a/solution.py
+++ b/solution.py
@@ -19,6 +19,7 @@
     0.23532515472880694, 0.09138881837358971, 0.6495583919191722,
     -0.6353990321145604, 0.8866636029850097, -0.22753693758818713,
 )
+MESH = pl.DeviceIdType.MESH
 NT = (((1,), (1,)), ((), ()))
 TN = (((0,), (0,)), ((), ()))
 
@@ -98,24 +99,195 @@
     return jnp.sum(v, 0, keepdims=True)
 
 
-def body(
-    x_ref, seg_ref, cot_ref, buf_a, buf_o, buf_u, buf_d,
-    lo_ref, ig_ref, ga_ref, go_ref, gu_ref, gd_ref,
-    piece, wqkv, wo, wup, wdn, small, rows_sm, upb,
-    qext, kext, qs, kk, vv, ctx, gctx, gm, lse, lse_t,
-    acc_o, acc_u, acc_d, acc_q, acc_b, acc_ub, acc_qv, tmp_t,
-):
+class Links:
+    def __init__(self):
+        dp, fsdp = lax.axis_index("dp"), lax.axis_index("fsdp")
+        self.at = {"x": dp // 2, "c": dp % 2, "z": fsdp // 2, "y": fsdp % 2}
+        self.dp, self.fsdp = dp, fsdp
+
+    def shifted(self, dim, by=1):
+        size = 4 if dim == "z" else 2
+        place = dict(self.at)
+        place[dim] = (place[dim] + by) % size
+        return place
+
+    def device(self, place):
+        return (place["x"] * 2 + place["c"], place["z"] * 2 + place["y"])
+
+    def partner(self, dim, by=1):
+        return self.device(self.shifted(dim, by))
+
+    def greet(self):
+        barrier = pltpu.get_barrier_semaphore()
+        others = [self.partner("x"), self.partner("c")]
+        others += [(self.dp, (self.fsdp + j) % 8) for j in range(1, 8)]
+        for other in others:
+            pl.semaphore_signal(barrier, inc=1, device_id=other, device_id_type=MESH)
+
+    def meet(self):
+        pl.semaphore_wait(pltpu.get_barrier_semaphore(), 9)
+
+
+def remote(src, dst, sems, slot, device):
+    return pltpu.make_async_remote_copy(
+        src_ref=src, dst_ref=dst, send_sem=sems[0].at[slot], recv_sem=sems[1].at[slot],
+        device_id=device, device_id_type=MESH,
+    )
+
+
+class Gather:
+    def __init__(self, links, buf, second, third, sems):
+        self.links, self.buf, self.sems = links, buf, sems
+        self.second, self.third = second, third
+
+    def slot(self, place):
+        return place["c"] * 16 + place[self.third] * 8 + place[self.second] * 4 + place["z"]
+
+    def run(self, place, level):
+        slot = self.slot(place)
+        size = (1, 4, 8)[level]
+        return self.buf.at[pl.ds(slot - slot % size, size)]
+
+    def hop(self, n, theirs):
+        links = self.links
+        here = links.at
+        if n < 3:
+            j = n + 1
+            other, back = links.shifted("z", j), links.shifted("z", 4 - j)
+            level = 0
+        elif n < 5:
+            other = back = links.shifted((self.second, self.third)[n - 3])
+            level = n - 2
+        else:
+            other = back = links.shifted("c")
+            if n == 5:
+                level = 1
+            else:
+                level = n - 5
+                dim = (self.second, self.third)[n - 6]
+                here = links.shifted(dim)
+                back = dict(back)
+                back[dim] = here[dim]
+        run = self.run(back if theirs else here, level)
+        return remote(run, run, self.sems, n, links.device(other))
+
+    def start(self, *stages):
+        for n in stages:
+            self.hop(n, False).start()
+
+    def arrive(self, *stages):
+        for n in stages:
+            self.hop(n, True).wait_recv()
+
+    def finish(self):
+        for n in range(8):
+            self.hop(n, False).wait_send()
+
+
+class Reduce:
+    def __init__(self, links, buf, land, second, third, sems):
+        self.links, self.buf, self.land, self.sems = links, buf, land, sems
+        self.second, self.third = second, third
+        at = links.at
+        self.base = (
+            0, at["c"] * 16, at["c"] * 16 + at[third] * 8,
+            at["c"] * 16 + at[third] * 8 + at[second] * 4,
+        )
+
+    def hop(self, n):
+        links = self.links
+        if n < 3:
+            dim = ("c", self.third, self.second)[n]
+            size, place = (16, 8, 4)[n], (0, 16, 24)[n]
+            start = self.base[n] + (1 - links.at[dim]) * size
+            other = links.partner(dim)
+        else:
+            j = n - 2
+            size, place = 1, 25 + n
+            start = self.base[3] + (links.at["z"] + j) % 4
+            other = links.partner("z", j)
+        return remote(
+            self.buf.at[pl.ds(start, size)], self.land.at[pl.ds(place, size)], self.sems, n, other
+        )
+
+    def start(self, *stages):
+        for n in stages:
+            self.hop(n).start()
+
+    def arrive(self, *stages):
+        for n in stages:
+            self.hop(n).wait_recv()
+
+    def add(self, n):
+        size, place = (16, 8, 4)[n], (0, 16, 24)[n]
+        start = self.base[n + 1]
+
+        def one(k, _):
+            total = self.buf[start + k].astype(F32) + self.land[place + k].astype(F32)
+            self.buf[start + k] = total.astype(BF16)
+            return 0
+
+        lax.fori_loop(0, size, one, 0)
+
+    def result(self):
+        total = self.buf[self.base[3] + self.links.at["z"]].astype(F32)
+        for k in range(28, 31):
+            total = total + self.land[k].astype(F32)
+        return total
+
+    def finish(self):
+        for n in range(6):
+            self.hop(n).wait_send()
+
+
+def body(linked, *refs):
+    x_ref, seg_ref, cot_ref = refs[:3]
+    in_a, in_o, in_u, in_d = refs[3:7]
+    lo_ref, ig_ref, ga_ref, go_ref, gu_ref, gd_ref = refs[7:13]
+    (
+        piece, wqkv, wo, wup, wdn, small, rows_sm, upb,
+        qext, kext, qs, kk, vv, ctx, gctx, gm, lse, lse_t,
+        acc_o, acc_u, acc_d, acc_b, acc_ub, acc_qv, tmp_t,
+    ) = refs[13:38]
     count, length = seg_ref.shape
     rows, width = x_ref.shape
+    if linked:
+        buf_a, buf_o, buf_u, buf_d, land_a, land_o, land_u, land_d = refs[38:46]
+        sems = refs[46:]
+        links = Links()
+        links.greet()
+        gather_o = Gather(links, buf_o, "x", "y", sems[2:4])
+        gather_u = Gather(links, buf_u, "y", "x", sems[4:6])
+        gather_d = Gather(links, buf_d, "x", "y", sems[6:8])
+        reduce_o = Reduce(links, buf_o, land_o, "x", "y", sems[8:10])
+        reduce_u = Reduce(links, buf_u, land_u, "y", "x", sems[10:12])
+        reduce_d = Reduce(links, buf_d, land_d, "x", "y", sems[12:14])
+        gathers, reduces = (gather_o, gather_u, gather_d), (reduce_o, reduce_u, reduce_d)
+        out_a, out_o, out_u, out_d = buf_a, buf_o, buf_u, buf_d
+    else:
+        buf_a, buf_o, buf_u, buf_d = in_a, in_o, in_u, in_d
+        out_a, out_o, out_u, out_d = ga_ref, go_ref, gu_ref, gd_ref
     n_dev, take, _ = buf_a.shape
     per = n_dev // GROUPS
     take_d = buf_d.shape[1]
 
+    def group_of(j):
+        if not linked:
+            return j
+        return ((links.at["x"] + j // 2) % 2) * 2 + (links.at["c"] + j % 2) % 2
+
+    def slot_of(second, g, p):
+        if not linked:
+            return g * per + p
+        x, c, z, y = g // 2, g % 2, p // 2, p % 2
+        if second == "x":
+            return c * 16 + y * 8 + x * 4 + z
+        return c * 16 + x * 8 + y * 4 + z
+
     wqkv[...] = jnp.zeros_like(wqkv)
-    wo[...] = jnp.zeros_like(wo)
     wup[...] = jnp.zeros_like(wup)
     wdn[...] = jnp.zeros_like(wdn)
-    acc_q[...] = jnp.zeros_like(acc_q)
+    wo[...] = jnp.zeros_like(wo)
     acc_o[...] = jnp.zeros_like(acc_o)
     acc_u[...] = jnp.zeros_like(acc_u)
     acc_d[...] = jnp.zeros_like(acc_d)
@@ -135,35 +307,58 @@
         kext[here, :] = k_t.T.astype(BF16)
         qext[here, :] = q_t.T.astype(BF16)
 
-    def gather(buf, group, cols, step):
-        align = 8 if step % 8 == 0 else 1
-
+    if linked:
+        buf_a[links.dp * 8 + links.fsdp] = in_a[...]
+        for one, ref in zip(gathers, (in_o, in_u, in_d)):
+            one.buf[one.slot(links.at)] = ref[...]
+
+        def near_a(j, theirs):
+            other, back = (links.fsdp + j) % 8, (links.fsdp + 8 - j) % 8
+            run = buf_a.at[pl.ds(links.dp * 8 + (back if theirs else links.fsdp), 1)]
+            return remote(run, run, sems[0:2], j - 1, (links.dp, back if theirs else other))
+
+        def far_a(kind, theirs):
+            x, c = links.at["x"], links.at["c"]
+            dim = ("c", "x", "c")[kind]
+            sent = (x if kind < 2 else 1 - x) * 2 + c
+            got = ((x * 2 + 1 - c), ((1 - x) * 2 + c), ((1 - x) * 2 + 1 - c))[kind]
+            run = buf_a.at[pl.ds((got if theirs else sent) * 8, 8)]
+            return remote(run, run, sems[0:2], 7 + kind, links.partner(dim))
+
+        links.meet()
+        for j in range(1, 8):
+            near_a(j, False).start()
+        gather_o.start(0, 1, 2)
+        for j in range(1, 8):
+            near_a(j, True).wait_recv()
+        far_a(0, False).start()
+        far_a(1, False).start()
+
+    def gather(buf, second, group, cols, step):
         def one(p, _):
-            at = pl.multiple_of(p * step, align)
-            piece[pl.ds(at, step), 0:cols] = buf[group * per + p].astype(F32)
+            at = pl.multiple_of(p * step, 8)
+            slot = group * per + p if second is None else slot_of(second, group, p)
+            piece[pl.ds(at, step), 0:cols] = buf[slot].astype(F32)
             return 0
 
         lax.fori_loop(0, per, one, 0)
 
-    def take_qkv(g, _):
-        gather(buf_a, g, 640, take)
+    def take_qkv(g):
+        gather(buf_a, None, g, 640, take)
         where = pl.ds(pl.multiple_of(inset(g), 64), 192)
         for part in range(3):
             wqkv[g, where, 256 * part : 256 * part + 192] = piece[
                 0:192, 192 * part : 192 * part + 192
             ].astype(BF16)
         small[g] = piece[0:192, 512:640].T[64:80]
-        return 0
-
-    lax.fori_loop(0, GROUPS, take_qkv, 0)
 
     def take_rest(g, _):
         where = pl.ds(pl.multiple_of(inset(g), 64), 192)
-        gather(buf_o, g, 768, take)
+        gather(buf_o, "x", g, 768, take)
         wo[g, 0:192, :] = piece[0:192, 0:768].astype(BF16)
-        gather(buf_u, g, 768, take)
+        gather(buf_u, "y", g, 768, take)
         wup[g, where, :] = piece[0:192, 0:768].astype(BF16)
-        gather(buf_d, g, 256, take_d)
+        gather(buf_d, "x", g, 256, take_d)
         upb[g] = piece[0:768, 128:256].T[64:72]
         w = piece[0:768, 0:192].astype(BF16)
 
@@ -176,9 +371,6 @@
             wdn[g, :, 64:256] = w
 
         return 0
-
-    lax.fori_loop(0, GROUPS, take_rest, 0)
-    rows_sm[...] = jnp.concatenate([small[g] for g in range(GROUPS)], -1)
 
     pad64 = jnp.zeros((1, 64), F32)
 
@@ -211,11 +403,80 @@
         ctx[g, here, :] = out.astype(BF16)
 
     def attend_step(i, _):
-        attend(i // count, i % count)
+        g = group_of(i // count)
+
+        if linked:
+
+            @pl.when(i == count)
+            def _():
+                far_a(0, True).wait_recv()
+
+            @pl.when(i == 2 * count)
+            def _():
+                far_a(1, True).wait_recv()
+                far_a(2, False).start()
+
+            @pl.when(i == 3 * count)
+            def _():
+                far_a(2, True).wait_recv()
+
+        @pl.when(i % count == 0)
+        def _():
+            take_qkv(g)
+
+        attend(g, i % count)
+
+        if linked:
+
+            @pl.when(i == 0)
+            def _():
+                gather_o.arrive(0, 1, 2)
+                gather_o.start(3, 5)
+                gather_u.start(0, 1, 2)
+                gather_d.start(0, 1, 2)
+
+            @pl.when(i == 2)
+            def _():
+                gather_u.arrive(0, 1, 2)
+                gather_u.start(3, 5)
+                gather_d.arrive(0, 1, 2)
+                gather_d.start(3, 5)
+                gather_o.arrive(3)
+                gather_o.start(4, 6)
+
+            @pl.when(i == 4)
+            def _():
+                gather_u.arrive(3)
+                gather_u.start(4, 6)
+                gather_d.arrive(3)
+                gather_d.start(4, 6)
+
+            @pl.when(i == 5)
+            def _():
+                gather_o.arrive(4)
+                gather_o.start(7)
+
+            @pl.when(i == 6)
+            def _():
+                gather_u.arrive(4)
+                gather_u.start(7)
+                gather_d.arrive(4)
+                gather_d.start(7)
+
         return 0
 
     lax.fori_loop(0, GROUPS * count, attend_step, 0)
     lse_t[...] = lse[...].T
+    if linked:
+        for one in gathers:
+            one.arrive(5, 6, 7)
+            one.finish()
+        for j in range(1, 8):
+            near_a(j, False).wait_send()
+        for kind in range(3):
+            far_a(kind, False).wait_send()
+    lax.fori_loop(0, GROUPS, take_rest, 0)
+    rows_sm[...] = jnp.concatenate([small[g] for g in range(GROUPS)], -1)
 
     block = 256
 
@@ -272,6 +533,34 @@
 
     lax.fori_loop(0, rows // block, ffn, 0)
 
+    def scatter(buf, second, group, cols, step):
+        def one(p, _):
+            at = pl.multiple_of(p * step, 8)
+            slot = group * per + p if second is None else slot_of(second, group, p)
+            buf[slot] = piece[pl.ds(at, step), 0:cols].astype(BF16)
+            return 0
+
+        lax.fori_loop(0, per, one, 0)
+
+    def give_rest(g, _):
+        piece[0:192, 0:768] = acc_o[g]
+        scatter(out_o, "x", g, 768, take)
+        piece[0:192, 0:768] = acc_u[g]
+        scatter(out_u, "y", g, 768, take)
+        ub = acc_ub[g, 0:1, :]
+        high = ub.astype(BF16).astype(F32)
+        full = jnp.concatenate([acc_d[g], high, ub - high, jnp.zeros((62, 768), F32)], 0)
+        piece[0:768, 0:256] = full.T
+        scatter(out_d, "x", g, 256, take_d)
+        return 0
+
+    lax.fori_loop(0, GROUPS, give_rest, 0)
+    if linked:
+        for one in reduces:
+            one.start(0)
+    for g in range(GROUPS):
+        small[g, 0:8] = acc_b[0:8, 192 * g : 192 * g + 192]
+
     def attend_back(g, b):
         here = pl.ds(pl.multiple_of(b * length, length), length)
         q = qs[g, here, :]
@@ -299,54 +588,117 @@
         acc_qv[g, 0:1, :] += col_sum(low_q.astype(F32))
         acc_qv[g, 1:2, :] += col_sum(low_v.astype(F32))
 
-    def back_step(g, _):
-        for b in range(count):
+    if linked:
+
+        def back_a(kind):
+            x, c = links.at["x"], links.at["c"]
+            sent = ((1 - x) * 2 + 1 - c, (1 - x) * 2 + c, x * 2 + 1 - c)[kind]
+            return remote(
+                buf_a.at[pl.ds(sent * 8, 8)], land_a.at[pl.ds(8 * kind, 8)],
+                sems[14:16], kind, links.partner(("c", "x", "c")[kind]),
+            )
+
+        def home_a(j):
+            other = (links.fsdp + j) % 8
+            return remote(
+                buf_a.at[pl.ds(links.dp * 8 + other, 1)], land_a.at[pl.ds(23 + j, 1)],
+                sems[14:16], 2 + j, (links.dp, other),
+            )
+
+        def join_a(g, first):
+            def one(p, _):
+                total = buf_a[g * per + p].astype(F32) + land_a[first + p].astype(F32)
+                buf_a[g * per + p] = total.astype(BF16)
+                return 0
+
+            lax.fori_loop(0, per, one, 0)
+
+    def back_step(i, _):
+        j = GROUPS - 1 - i
+        g = group_of(j)
+        attend_back(g, 0)
+
+        if linked:
+
+            @pl.when(i == 2)
+            def _():
+                for one in reduces:
+                    one.arrive(1)
+                    one.add(1)
+                    one.start(2)
+
+        for b in range(1, count):
             attend_back(g, b)
         mixed = gm[...]
         at = pl.ds(pl.multiple_of(edge(g), 128), 256)
         xw = x_ref[:, at]
         tmp_t[...] = dot(xw.T, mixed)
-        acc_q[g] = tmp_t[pl.ds(pl.multiple_of(inset(g), 64), 192), :]
         ig_ref[:, at] += dot_nt(mixed, wqkv[g])
-        return 0
-
-    lax.fori_loop(0, GROUPS, back_step, 0)
-
-    def scatter(buf, group, cols, step):
-        align = 8 if step % 8 == 0 else 1
-
-        def one(p, _):
-            at = pl.multiple_of(p * step, align)
-            buf[group * per + p] = piece[pl.ds(at, step), 0:cols].astype(buf.dtype)
-            return 0
-
-        lax.fori_loop(0, per, one, 0)
-
-    for g in range(GROUPS):
+        where = pl.ds(pl.multiple_of(inset(g), 64), 192)
         for part in range(3):
-            piece[0:192, 192 * part : 192 * part + 192] = acc_q[g, :, 256 * part : 256 * part + 192]
-        mine = jnp.concatenate(
-            [acc_qv[g, 0:2, 0:192], acc_b[2:8, 192 * g : 192 * g + 192]], 0
-        )
+            piece[0:192, 192 * part : 192 * part + 192] = tmp_t[where, 256 * part : 256 * part + 192]
+        mine = jnp.concatenate([acc_qv[g, 0:2, 0:192], small[g, 2:8]], 0)
         high = mine.astype(BF16).astype(F32)
         side = jnp.concatenate([high, mine - high, jnp.zeros((112, 192), F32)], 0)
         piece[0:192, 576:640] = side.T[:, 0:64]
-        scatter(ga_ref, g, 640, take)
-        piece[0:192, 0:768] = acc_o[g]
-        scatter(go_ref, g, 768, take)
-        piece[0:192, 0:768] = acc_u[g]
-        scatter(gu_ref, g, 768, take)
-        ub = acc_ub[g, 0:1, :]
-        high = ub.astype(BF16).astype(F32)
-        full = jnp.concatenate([acc_d[g], high, ub - high, jnp.zeros((62, 768), F32)], 0)
-        piece[0:768, 0:256] = full.T
-        scatter(gd_ref, g, 256, take_d)
-
-
-def layer(tokens, segment_ids, cotangent, buf_a, buf_o, buf_u, buf_d):
+        scatter(out_a, None, g, 640, take)
+
+        if linked:
+
+            @pl.when(i == 0)
+            def _():
+                back_a(0).start()
+                for one in reduces:
+                    one.arrive(0)
+                    one.add(0)
+                    one.start(1)
+
+            @pl.when(i == 1)
+            def _():
+                back_a(0).wait_recv()
+                join_a(g, 0)
+                back_a(1).start()
+
+            @pl.when(i == 2)
+            def _():
+                back_a(2).start()
+                for one in reduces:
+                    one.arrive(2)
+                    one.add(2)
+                    one.start(3, 4, 5)
+
+            @pl.when(i == 3)
+            def _():
+                back_a(1).wait_recv()
+                back_a(2).wait_recv()
+                join_a(g, 8)
+                join_a(g, 16)
+                for k in range(1, 8):
+                    home_a(k).start()
+
+        return 0
+
+    lax.fori_loop(0, GROUPS, back_step, 0)
+    if linked:
+        for one, ref in zip(reduces, (go_ref, gu_ref, gd_ref)):
+            one.arrive(3, 4, 5)
+            ref[...] = one.result()
+            one.finish()
+        for k in range(3):
+            back_a(k).wait_send()
+        total = buf_a[links.dp * 8 + links.fsdp].astype(F32)
+        for k in range(1, 8):
+            home_a(k).wait_recv()
+            total = total + land_a[23 + k].astype(F32)
+        ga_ref[...] = total
+        for k in range(1, 8):
+            home_a(k).wait_send()
+
+
+def layer(linked, tokens, segment_ids, cotangent, a, o, u, d):
     count, length, width = tokens.shape
     rows = count * length
-    grad = lambda buf: jax.ShapeDtypeStruct(buf.shape, BF16)
+    kind = F32 if linked else BF16
     scratch = [
         pltpu.VMEM((768, 768), F32),
         pltpu.VMEM((4, 256, 768), BF16),
@@ -369,41 +721,56 @@
         pltpu.VMEM((4, 192, 768), F32),
         pltpu.VMEM((4, 192, 768), F32),
         pltpu.VMEM((4, 192, 768), F32),
-        pltpu.VMEM((4, 192, 768), F32),
         pltpu.VMEM((8, 768), F32),
         pltpu.VMEM((4, 8, 768), F32),
         pltpu.VMEM((4, 8, 256), F32),
         pltpu.VMEM((256, 768), F32),
     ]
+    params = {"vmem_limit_bytes": 62 * 1024 * 1024}
+    if linked:
+        scratch += [pltpu.VMEM((32,) + v.shape, BF16) for v in (a, o, u, d)]
+        scratch += [pltpu.VMEM((31,) + v.shape, BF16) for v in (a, o, u, d)]
+        for n in (10, 8, 8, 8, 6, 6, 6, 10):
+            scratch += [pltpu.SemaphoreType.DMA((n,)), pltpu.SemaphoreType.DMA((n,))]
+        params |= {"collective_id": 0, "has_side_effects": True}
     vm = pl.BlockSpec(memory_space=pltpu.VMEM)
     return pl.pallas_call(
-        body,
+        partial(body, linked),
         out_shape=(
             jax.ShapeDtypeStruct((rows, width), BF16),
             jax.ShapeDtypeStruct((rows, width), F32),
-            grad(buf_a), grad(buf_o), grad(buf_u), grad(buf_d),
+            *(jax.ShapeDtypeStruct(v.shape, kind) for v in (a, o, u, d)),
         ),
         in_specs=[vm] * 7,
         out_specs=[vm] * 6,
         scratch_shapes=scratch,
-        compiler_params=pltpu.CompilerParams(vmem_limit_bytes=62 * 1024 * 1024),
-    )(tokens.reshape(rows, width), segment_ids, cotangent.reshape(rows, width), buf_a, buf_o, buf_u, buf_d)
-
-
-def local(tokens, segment_ids, qkv_weight, out_weight, up_weight, down_weight, biases, up_bias, gains, cotangent):
+        compiler_params=pltpu.CompilerParams(**params),
+    )(tokens.reshape(rows, width), segment_ids, cotangent.reshape(rows, width), a, o, u, d)
+
+
+def local(
+    linked, tokens, segment_ids, qkv_weight, out_weight, up_weight, down_weight,
+    biases, up_bias, gains, cotangent,
+):
     axes = ("dp", "fsdp")
     take, take_d = qkv_weight.shape[0], down_weight.shape[0]
     zeros = lambda r, c: jnp.zeros((r, c), BF16)
     pack_a = jnp.concatenate([qkv_weight, biases.T, gains.T, zeros(take, 56)], 1)
     pack_d = jnp.concatenate([down_weight, up_bias[:, None], zeros(take_d, 63)], 1)
-    gather = lambda v: lax.all_gather(v, axes, axis=0, tiled=True).reshape(32, -1, v.shape[1])
-    out, ig, ga, go, gu, gd = layer(
-        tokens, segment_ids, cotangent, gather(pack_a), gather(out_weight), gather(up_weight), gather(pack_d)
-    )
-    total = lambda v: lax.psum_scatter(
-        v.reshape(-1, v.shape[2]).astype(F32), axes, scatter_dimension=0, tiled=True
-    )
-    ga, go, gu, gd = total(ga), total(go), total(gu), total(gd)
+    shards = (pack_a, out_weight, up_weight, pack_d)
+    if not linked:
+        shards = [
+            lax.all_gather(v, axes, axis=0, tiled=True).reshape(32, -1, v.shape[1]) for v in shards
+        ]
+    out, ig, *grads = layer(linked, tokens, segment_ids, cotangent, *shards)
+    if not linked:
+        grads = [
+            lax.psum_scatter(
+                v.reshape(-1, v.shape[2]).astype(F32), axes, scatter_dimension=0, tiled=True
+            )
+            for v in grads
+        ]
+    ga, go, gu, gd = grads
     side = (ga[:, 576:584] + ga[:, 584:592]).T
     return (
         out.reshape(tokens.shape), ig.reshape(tokens.shape),
@@ -415,4 +782,7 @@
     row, col = P(("dp", "fsdp")), P(None, ("dp", "fsdp"))
     in_specs = (row, row, row, row, row, row, col, row, col, row)
     out_specs = (row, row, row, row, row, row, col, row, col)
-    return jax.shard_map(local, mesh=mesh, in_specs=in_specs, out_specs=out_specs, check_vma=False)
+    linked = (mesh.shape["dp"], mesh.shape["fsdp"]) == (4, 8)
+    return jax.shard_map(
+        partial(local, linked), mesh=mesh, in_specs=in_specs, out_specs=out_specs, check_vma=False
+    )

time: 727 us -> 145 us (0.20)
  waiting for transfers between devices: 522 us -> 0 us
  blocking collectives: 80.9 us -> 0 us
  Pallas kernels: 86.7 us -> 128 us
  between operations: 14.2 us -> 0.68 us
    reduce_scatter x3 -> x0, waiting for transfers between devices: 310 us -> none  [local(): lax.psum_scatter(v.reshape(-1, v.shape[2]).astype(F32), axes, scatter_dim...]
    unnamed x8 -> x0, waiting for transfers between devices: 124 us -> none
    all_gather x3 -> x0, waiting for transfers between devices: 88.2 us -> none  [local(): lax.all_gather(v, axes, axis=0, tiled=True).reshape(32, -1, v.shape[1])]
    all_gather x1 -> x0, blocking collectives: 80.9 us -> none  [local(): lax.all_gather(v, axes, axis=0, tiled=True).reshape(32, -1, v.shape[1])]
    pallas_call x1, Pallas kernels: 86.7 us -> 128 us  [layer(): pl.pallas_call(partial(body, linked), out_shape=(jax.ShapeDtypeStruct((ro...]
  transfers between devices with their start and end apart: 7 -> 0, of which waited for: 6 -> 0; matrix products, arithmetic and copies ran while one was open for 2% -> 0% of each run, Pallas kernels for 0% -> 0%
where the time goes in v2:
time: 145 us
  Pallas kernels  128 us (88%)
  local copies, waits for them, and re-layouts  10.8 us (7%)
  other arithmetic  5.39 us (4%)
    pallas_call x1, Pallas kernels, layer(): pl.pallas_call(partial(body, linked), out_shape=(jax.ShapeDtypeStruct((ro...  128 us
    unnamed x20, local copies, waits for them, and re-layouts  9.84 us

profile of v2, /device:TPU:0, one launch (start us, length us, event | category | flops | bytes accessed | tf_op | source)
XLA Modules:
  0.0 144.9 jit_solution(7321956426865207286)
XLA Ops:
  0.7 0.1 pad.2.clone
  0.7 0.1 pad.6.clone
  0.8 0.8 copy.24
  1.6 0.7 copy.25
  2.3 1.4 maximum_maximum_fusion.1.refs_3_
  3.8 0.8 copy.26
  4.5 1.5 %maximum_maximum_fusion.refs_6_ = bf16[96,256]{1,0:T(8,128)(2,1)} fusion(bf16[96,1]{1,0:T(8,128)(2,1)S(1)} %copy.26, bf16[96,192]{1,0:T(8,128)(2,1)} %param.15, bf16[256]{0:T(256)(128)(2,1)S(1)} %pad.2.clone), kind=kLoop, calls=%fused_computation | loop fusion | flops 147456 | bytes 86720 | tf_op jit(solution)/shard_map/concatenate | solution.py:759
  6.0 128.0 %shard_map.169 = (bf16[1024,768]{1,0:T(8,128)(2,1)}, f32[1024,768]{1,0:T(8,128)}, f32[24,640]{1,0:T(8,128)}, f32[24,768]{1,0:T(8,128)}, f32[24,768]{1,0:T(8,128)}, /*index=5*/f32[96,256]{1,0:T(8,128)}) custom-call(bf16[1024,768]{1,0:T(8,128)(2,1)} %bitcast.13, s32[2,512]{1,0:T(2,128)} %refs_1_.1, bf16[1024,768]{1,0:T(8,128)(2,1)} %bitcast.14, ...), custom_call_target="tpu_custom_call" | custom-call | tf_op jit(solution)/shard_map/pallas_call | solution.py:737
  134.0 1.6 %add_reduce_fusion = f32[96]{0:T(128)} fusion(f32[96,256]{1,0:T(8,128)} %get-tuple-element.20), kind=kLoop, calls=%fused_computation.1 | loop fusion | flops 96 | bytes 1152 | tf_op jit(solution)/shard_map/add | solution.py:777
  135.6 0.9 add_bitcast_fusion
  136.5 0.7 copy.27
  137.1 0.1 slice.33
  137.2 0.6 copy.28
  137.9 0.0 copy-start
  137.9 2.8 %copy.35 = bf16[2,512,768]{2,1,0:T(8,128)(2,1)} copy(bf16[2,512,768]{2,1,0:T(8,128)(2,1)} %bitcast.15) | data formatting | bytes 3145728
  140.7 0.0 copy-done
  140.7 0.0 copy-start.2
  140.7 0.0 copy-start.4
  140.7 0.0 copy-start.3
  140.7 0.0 copy-start.1
  140.7 1.7 %copy.36 = f32[2,512,768]{2,1,0:T(8,128)} copy(f32[2,512,768]{2,1,0:T(8,128)S(1)} %bitcast.12) | data formatting | bytes 6291456
  142.3 0.0 copy-done.2
  142.4 0.6 copy.37
  143.0 0.0 copy-done.4
  143.0 0.6 copy.38
  143.6 0.0 copy-done.3
  143.6 0.6 copy.39
  144.2 0.0 copy-done.1
  144.3 0.6 copy.40
  (2 shorter events, 0.0 us)
Async XLA Ops:
  137.9 2.8 %copy-start = (f32[1024,768]{1,0:T(8,128)S(1)}, f32[1024,768]{1,0:T(8,128)}, u32[]{:S(2)}) copy-start(f32[1024,768]{1,0:T(8,128)} %get-tuple-element.16) | copy-start | bytes 9437188
  140.7 1.7 %copy-start.2 = (f32[24,640]{1,0:T(8,128)S(1)}, f32[24,640]{1,0:T(8,128)}, u32[]{:S(2)}) copy-start(f32[24,640]{1,0:T(8,128)} %get-tuple-element.17) | copy-start | bytes 184324
  140.7 2.3 %copy-start.4 = (f32[24,768]{1,0:T(8,128)S(1)}, f32[24,768]{1,0:T(8,128)}, u32[]{:S(2)}) copy-start(f32[24,768]{1,0:T(8,128)} %get-tuple-element.51) | copy-start | bytes 221188
  140.7 2.9 %copy-start.3 = (f32[24,768]{1,0:T(8,128)S(1)}, f32[24,768]{1,0:T(8,128)}, u32[]{:S(2)}) copy-start(f32[24,768]{1,0:T(8,128)} %get-tuple-element.52) | copy-start | bytes 221188
  140.7 3.6 %copy-start.1 = (f32[96,256]{1,0:T(8,128)S(1)}, f32[96,256]{1,0:T(8,128)}, u32[]{:S(2)}) copy-start(f32[96,256]{1,0:T(8,128)} %get-tuple-element.20) | copy-start | bytes 294916
